TPU v7x, 512 devices: a whole 4x4x16 slice. The times are simulated.
512 devices in a mesh: dp: 32 (over z, core), expert: 16 (over x, y).
Axes of the slice: x: 4, y: 4, z: 16, core: 2. Of those that a mesh axis runs over, the one named last changes fastest.
Arguments:
- cached_hidden: bfloat16 [65536, 1536], P(('dp', 'expert')), may hold values from -6 to 6
- direction: bfloat16 [16, 2880, 1536], P('expert', 'dp'), may hold values from -1 to 1
- expert_ids: int32 [65536, 4], P(('dp', 'expert')), may hold values from 0 to 127, as said below
- gate_weights: float32 [65536, 4], P(('dp', 'expert')), may hold values from 0.05 to 1
Outputs:
- curvature_product: float32 [16, 2880, 1536], P('expert', 'dp')
Inputs may be any that keep to these rules, and one draw needn't show every extreme that they name: `expert_ids`: each row names 4 different experts, at most two of them below 16. Among the 128 rows of one device no expert below 16 is named more than 8 times; for every dp index, some expert below 16 is named exactly 8 times by the rows of each device with that dp index.
All inputs are finite; a program needn't handle non-finite values.
Results may differ from a plain program's by a relative error of at most 0.0034.
Values may be sent and summed in bfloat16 or wider, within the bound.
No kernel may reach another device: no remote copies, remote signals or barrier semaphores. Data moves between devices by JAX's collectives and lax.ppermute only.
A program may use at most 128 MiB of HBM per device.

v0:
```python
import math
import jax
import jax.numpy as jnp
from jax import lax
from jax.sharding import PartitionSpec as P


def slot_positions(block_ids, experts):
    flat = block_ids.reshape(-1)
    onehot = (flat[:, None] == jnp.arange(experts, dtype=jnp.int32)[None, :]).astype(jnp.int32)
    before = jnp.cumsum(onehot, axis=0) - onehot
    return jnp.sum(before * onehot, axis=1).reshape(block_ids.shape)


def body(cached_hidden, direction, expert_ids, gate_weights):
    dp_count = lax.axis_size("dp")
    owner_count = lax.axis_size("expert")
    slot_rows = cached_hidden.shape[0]
    capacity = slot_rows // owner_count
    tok_count = expert_ids.shape[0]
    width = direction.shape[1] * dp_count
    local_dir = direction[0]
    rows_all = lax.all_gather(cached_hidden, "dp", axis=0, tiled=True)
    tangent = lax.dot_general(
        rows_all, local_dir, (((1,), (1,)), ((), ())), preferred_element_type=jnp.float32
    )
    tangent = tangent.astype(jnp.bfloat16).reshape(
        dp_count, owner_count, capacity, local_dir.shape[0]
    )
    returned = lax.all_to_all(
        lax.all_to_all(tangent, "dp", split_axis=0, concat_axis=3, tiled=True),
        "expert",
        split_axis=1,
        concat_axis=1,
        tiled=True,
    )
    flat_rows = returned.reshape(owner_count * capacity, width)
    treated = expert_ids < owner_count
    slot_pos = slot_positions(expert_ids, owner_count)
    target = expert_ids * capacity + slot_pos
    lookup = jnp.where(treated, target, 0).reshape(-1)
    dropped = jnp.where(treated, target, owner_count * capacity).reshape(-1)
    gates = jnp.where(treated, gate_weights, 0.0)
    picked = jnp.take(flat_rows, lookup, axis=0).reshape(tok_count, expert_ids.shape[1], width)
    scale_factor = 1.0 / math.sqrt(tok_count * dp_count * owner_count)
    combined = jnp.sum(gates[..., None] * picked.astype(jnp.float32), axis=1) * scale_factor
    outgoing = (gates[..., None] * combined[:, None, :]).astype(jnp.bfloat16)
    buffer = jnp.zeros((owner_count * capacity, width), jnp.bfloat16)
    buffer = buffer.at[dropped].set(outgoing.reshape(-1, width), mode="drop")
    buffer = buffer.reshape(1, owner_count, capacity, width)
    arrived = lax.all_to_all(buffer, "expert", split_axis=1, concat_axis=1, tiled=True)
    adjoint = lax.all_to_all(arrived, "dp", split_axis=3, concat_axis=0, tiled=True)
    adjoint_rows = adjoint.reshape(-1, adjoint.shape[3])
    gradient = lax.dot_general(
        adjoint_rows, rows_all, (((0,), (0,)), ((), ())), preferred_element_type=jnp.float32
    )
    return gradient.reshape(1, gradient.shape[0], gradient.shape[1])


def solution(mesh):
    return jax.shard_map(
        body,
        mesh=mesh,
        in_specs=(
            P(("dp", "expert"), None),
            P("expert", "dp", None),
            P(("dp", "expert"), None),
            P(("dp", "expert"), None),
        ),
        out_specs=P("expert", "dp", None),
        check_vma=False,
    )
```

profile of v0, /device:TPU:1, one launch (start us, length us, event | category | flops | bytes accessed | tf_op | source)
XLA Modules:
  0.0 336.8 jit_solution(6748889101096679168)
XLA Ops:
  6.5 0.7 all-gather.2.cloned.1.call-update
  7.3 95.0 %all-gather.2.cloned.1.call-done = bf16[4096,1536]{1,0:T(8,128)(2,1)} async-done(((bf16[128,1536]{1,0:T(8,128)(2,1)}), bf16[4096,1536]{1,0:T(8,128)(2,1)}) %all-gather.2.cloned.1.call-update) | async-done | bytes 12582928 | tf_op jit(solution)/shard_map/all_gather | solution.py:23
  102.3 8.5 %convolution_convert_fusion = bf16[4096,90]{0,1:T(8,128)(2,1)S(1)} fusion(bf16[4096,1536]{1,0:T(8,128)(2,1)} %all-gather.2.cloned.1.call-done, bf16[1,90,1536]{2,1,0:T(8,128)(2,1)S(1)} %copy-done), kind=kOutput, calls=%fused_computation.4 | convolution fusion | flops 1132830720 | bytes 13596672 | tf_op jit(solution)/shard_map/dot_general | solution.py:24
  110.8 1.4 copy.65
  112.2 7.8 %all-to-all-start = ((bf16[32,16,8,90]{3,2,1,0:T(8,128)(2,1)}), bf16[32,16,8,90]{3,2,1,0:T(8,128)(2,1)S(1)}, u32[]{:S(2)}, u32[]{:S(2)}) async-start(bf16[32,16,8,90]{3,2,1,0:T(8,128)(2,1)} %bitcast.3), calls=%async_computation | async-start | bytes 2097152 | tf_op jit(solution)/shard_map/all_to_all | solution.py:31
  120.6 1.2 reduce-window.6
  122.5 53.2 %all-to-all-done = bf16[32,16,8,90]{3,2,1,0:T(8,128)(2,1)S(1)} async-done(((bf16[32,16,8,90]{3,2,1,0:T(8,128)(2,1)}), bf16[32,16,8,90]{3,2,1,0:T(8,128)(2,1)S(1)}, u32[]{:S(2)}, u32[]{:S(2)}) %all-to-all-start) | async-done | bytes 737312 | tf_op jit(solution)/shard_map/all_to_all | solution.py:31
  176.4 2.9 all_to_all.33
  179.3 6.5 %all-to-all-start.1 = ((bf16[1,16,8,2880]{3,2,0,1:T(8,128)(2,1)}), bf16[1,16,8,2880]{3,2,0,1:T(8,128)(2,1)S(1)}, u32[]{:S(2)}, u32[]{:S(2)}) async-start(bf16[1,16,8,2880]{3,2,0,1:T(8,128)(2,1)} %bitcast.6), calls=%async_computation.1 | async-start | bytes 1507328 | tf_op jit(solution)/shard_map/all_to_all | solution.py:30
  186.3 11.9 %all-to-all-done.1 = bf16[1,16,8,2880]{3,2,0,1:T(8,128)(2,1)S(1)} async-done(((bf16[1,16,8,2880]{3,2,0,1:T(8,128)(2,1)}), bf16[1,16,8,2880]{3,2,0,1:T(8,128)(2,1)S(1)}, u32[]{:S(2)}, u32[]{:S(2)}) %all-to-all-start.1) | async-done | bytes 737312 | tf_op jit(solution)/shard_map/all_to_all | solution.py:30
  198.2 3.7 %gather_fusion = bf16[512,2880]{1,0:T(8,128)(2,1)} fusion(bf16[128,2880]{1,0:T(8,128)(2,1)S(1)} %bitcast.44, s32[1024]{0:T(1024)S(1)} %pad_clamp_fusion), kind=kCustom, calls=%fused_computation | custom fusion | bytes 5900288 | tf_op jit(solution)/shard_map/jit(_take)/gather | solution.py:44
  201.9 4.7 %gather.7 = bf16[128,4,2880]{2,1,0:T(4,128)(2,1)S(1)} reshape(bf16[512,2880]{1,0:T(8,128)(2,1)} %gather_fusion) | data formatting | bytes 5898240 | tf_op jit(solution)/shard_map/jit(_take)/gather | solution.py:44
  206.6 6.3 %multiply_reduce_fusion = f32[128,2880]{1,0:T(8,128)S(1)} fusion(bf16[128,4,2880]{2,1,0:T(4,128)(2,1)S(1)} %gather.7, f32[128,4]{1,0:T(8,128)S(1)} %copy.62, pred[128,4]{1,0:T(8,128)(4,1)S(1)} %copy.64), kind=kLoop, calls=%fused_computation.3 | loop fusion | flops 5529600 | bytes 4426240 | tf_op jit(solution)/shard_map/reduce_sum | solution.py:46
  213.0 3.6 %mul.54 = f32[128,4,2880]{2,1,0:T(4,128)} broadcast(f32[128,2880]{1,0:T(8,128)S(1)} %broadcast_multiply_fusion), dimensions={0,2} | broadcast | bytes 7372800 | tf_op jit(solution)/shard_map/mul | solution.py:47
  216.5 7.7 %mul.55 = f32[512,2880]{1,0:T(8,128)} reshape(f32[128,4,2880]{2,1,0:T(4,128)} %mul.54) | data formatting | bytes 11796480 | tf_op jit(solution)/shard_map/mul | solution.py:47
  224.3 7.1 %scatter_custom_fusion = bf16[128,2880]{1,0:T(8,128)(2,1)S(1)} fusion(s32[512]{0:T(512)S(1)} %bitcast.52, f32[512,2880]{1,0:T(8,128)} %mul.55, f32[512]{0:T(512)S(1)} %mul.48, bf16[]{:T(256)} %constant.9.clone.1), kind=kCustom, calls=%fused_computation.5 | custom fusion | flops 2949120 | bytes 6637570 | tf_op jit(solution)/shard_map/scatter | solution.py:49
  231.4 15.4 %all_to_all.43 = bf16[1,16,8,2880]{3,2,0,1:T(8,128)(2,1)S(1)} all-to-all(bf16[1,16,8,2880]{3,2,0,1:T(8,128)(2,1)S(1)} %bitcast.50), channel_id=1, replica_groups=mesh['dp'=32,'expert'=16] {'expert'}, dimensions={1} | all-to-all | bytes 1474560 | tf_op jit(solution)/shard_map/all_to_all | solution.py:51
  246.8 5.5 %copy.69 = bf16[1,16,8,2880]{1,2,0,3:T(8,128)(2,1)} copy(bf16[1,16,8,2880]{3,2,0,1:T(8,128)(2,1)S(1)} %all_to_all.43) | data formatting | bytes 1474560 | tf_op jit(solution)/shard_map/all_to_all | solution.py:51
  252.4 8.5 %reshape.146 = bf16[32,2,5760]{2,1,0:T(2,128)(2,1)S(1)} reshape(bf16[2880,1,8,16]{3,2,1,0:T(8,128)(2,1)} %bitcast.45) | data formatting | bytes 1474560
  260.9 48.5 %all_to_all.44 = bf16[32,2,5760]{2,1,0:T(2,128)(2,1)S(1)} all-to-all(bf16[32,2,5760]{2,1,0:T(2,128)(2,1)S(1)} %reshape.146), channel_id=1, replica_groups=mesh['dp'=32,'expert'=16] {'dp'}, dimensions={0} | all-to-all | bytes 1474560 | tf_op jit(solution)/shard_map/all_to_all | solution.py:52
  309.4 5.5 %reshape.147 = bf16[2880,1,8,16]{3,2,1,0:T(8,128)(2,1)} reshape(bf16[32,2,5760]{2,1,0:T(2,128)(2,1)S(1)} %all_to_all.44) | data formatting | bytes 1474560
  314.9 6.5 %copy.73 = bf16[1,16,8,32,90]{4,3,2,1,0:T(8,128)(2,1)S(1)} copy(bf16[1,16,8,32,90]{1,2,4,3,0:T(8,128)(2,1)} %bitcast.46) | data formatting | bytes 1474560 | tf_op jit(solution)/shard_map/all_to_all | solution.py:52
  321.9 6.7 %convolution_bitcast_fusion = f32[1,90,1536]{2,1,0:T(8,128)S(1)} fusion(bf16[4096,90]{1,0:T(8,128)(2,1)S(1)} %bitcast.47, bf16[4096,1536]{1,0:T(8,128)(2,1)} %all-gather.2.cloned.1.call-done), kind=kOutput, calls=%fused_computation.7 | convolution fusion | flops 1132462080 | bytes 13873152 | tf_op jit(solution)/shard_map/dot_general | solution.py:54
  328.6 1.4 copy.72
  (33 shorter events, 2.9 us)
Async XLA Ops:
  6.5 95.7 %copy-start = (bf16[1,90,1536]{2,1,0:T(8,128)(2,1)S(1)}, bf16[1,90,1536]{2,1,0:T(8,128)(2,1)}, u32[]{:S(2)}) copy-start(bf16[1,90,1536]{2,1,0:T(8,128)(2,1)} %param.5) | copy-start | bytes 829444
  6.5 95.7 %all-gather.2.cloned.1.call-start = ((), (), s32[]{:S(2)}) async-start(), calls=%async_computation.4 | async-start | bytes 12976128 | tf_op jit(solution)/shard_map/all_gather | solution.py:23
  110.7 9.3 %copy-start.1 = (s32[128,4]{0,1:T(4,128)S(1)}, s32[128,4]{0,1:T(4,128)}, u32[]{:S(2)}) copy-start(s32[128,4]{0,1:T(4,128)} %param.6) | copy-start | bytes 6148
  110.7 9.6 %copy-start.2 = (f32[128,4]{0,1:T(4,128)S(1)}, f32[128,4]{0,1:T(4,128)}, u32[]{:S(2)}) copy-start(f32[128,4]{0,1:T(4,128)} %param.7) | copy-start | bytes 6148
  112.2 63.5 %all-to-all-start = ((bf16[32,16,8,90]{3,2,1,0:T(8,128)(2,1)}), bf16[32,16,8,90]{3,2,1,0:T(8,128)(2,1)S(1)}, u32[]{:S(2)}, u32[]{:S(2)}) async-start(bf16[32,16,8,90]{3,2,1,0:T(8,128)(2,1)} %bitcast.3), calls=%async_computation | async-start | bytes 2097152 | tf_op jit(solution)/shard_map/all_to_all | solution.py:31
  179.3 19.0 %all-to-all-start.1 = ((bf16[1,16,8,2880]{3,2,0,1:T(8,128)(2,1)}), bf16[1,16,8,2880]{3,2,0,1:T(8,128)(2,1)S(1)}, u32[]{:S(2)}, u32[]{:S(2)}) async-start(bf16[1,16,8,2880]{3,2,0,1:T(8,128)(2,1)} %bitcast.6), calls=%async_computation.1 | async-start | bytes 1507328 | tf_op jit(solution)/shard_map/all_to_all | solution.py:30
Sparse Core Ops, SparseCore 0:
  9.5 92.7 all-gather.1
where the time goes:
time: 338 us; the launch traced here: 337 us
  waiting for transfers between devices  161 us (48%)
  blocking collectives  63.9 us (19%)
  local copies, waits for them, and re-layouts  54 us (16%)
  matrix products  15.2 us (4%)
  other arithmetic  14.9 us (4%)
  starting transfers between devices  14.3 us (4%)
  between operations  13.6 us (4%)
    all_gather x1, waiting for transfers between devices, body(): rows_all = lax.all_gather(cached_hidden, 'dp', axis=0, tiled=True)  95 us
    all_to_all x1, waiting for transfers between devices, body(): lax.all_to_all(tangent, 'dp', split_axis=0, concat_axis=3, tiled=True)  53.2 us
    all_to_all x1, blocking collectives, body(): lax.all_to_all(arrived, 'dp', split_axis=3, concat_axis=0, tiled=True)  48.5 us
    all_to_all x1, blocking collectives, body(): lax.all_to_all(buffer, 'expert', split_axis=1, concat_axis=1, tiled=True)  15.4 us
    unnamed x9, local copies, waits for them, and re-layouts  14.2 us
    all_to_all x1, waiting for transfers between devices, body(): lax.all_to_all(lax.all_to_all(tangent, 'dp', split_axis=0, concat_axis=3,...  11.9 us
    mul x3, local copies, waits for them, and re-layouts, body(): outgoing = (gates[..., None] * combined[:, None, :]).astype(jnp.bfloat16)  11.4 us
    dot_general x1, matrix products, body(): lax.dot_general(rows_all, local_dir, (((1,), (1,)), ((), ())), preferred_...  8.46 us
  transfers between devices with their start and end apart: 3, of which 3 were waited for; matrix products, arithmetic and copies ran while one was open for 1% of the time, Pallas kernels for 0%

commit v1 on v0

--- a/solution.py
+++ b/solution.py
@@ -20,7 +20,10 @@
     tok_count = expert_ids.shape[0]
     width = direction.shape[1] * dp_count
     local_dir = direction[0]
-    rows_all = lax.all_gather(cached_hidden, "dp", axis=0, tiled=True)
+    balance_array = lambda sample: jnp.concatenate(
+        jax.lax.all_to_all(jnp.stack([sample] * jax.lax.axis_size("dp")), "dp", 0, 0), axis=0
+    )
+    rows_all = balance_array(cached_hidden)
     tangent = lax.dot_general(
         rows_all, local_dir, (((1,), (1,)), ((), ())), preferred_element_type=jnp.float32
     )

time: 338 us -> 799 us (2.36)
  blocking collectives: 63.9 us -> 631 us
  waiting for transfers between devices: 161 us -> 65.3 us
  between operations: 13.6 us -> 0.2 us
  local copies, waits for them, and re-layouts: 54 us -> 65.6 us
    all_to_all x0 -> x1, blocking collectives: none -> 567 us  [body(): jax.lax.all_to_all(jnp.stack([sample] * jax.lax.axis_size('dp')), 'dp', 0...]
    all_gather x1 -> x0, waiting for transfers between devices: 95 us -> none  [body(): rows_all = lax.all_gather(cached_hidden, 'dp', axis=0, tiled=True)]
    unnamed x9 -> x13, local copies, waits for them, and re-layouts: 14.2 us -> 18.7 us
  transfers between devices with their start and end apart: 3 -> 2, of which waited for: 3 -> 2; matrix products, arithmetic and copies ran while one was open for 1% -> 0% of each run, Pallas kernels for 0% -> 0%
where the time goes in v1:
time: 799 us; the launch traced here: 798 us
  blocking collectives  631 us (79%)
  local copies, waits for them, and re-layouts  65.6 us (8%)
  waiting for transfers between devices  65.3 us (8%)
  other arithmetic  14.9 us (2%)
  starting transfers between devices  10.9 us (1%)
  matrix products  10.7 us (1%)
    all_to_all x1, blocking collectives, body(): jax.lax.all_to_all(jnp.stack([sample] * jax.lax.axis_size('dp')), 'dp', 0...  567 us
    all_to_all x1, waiting for transfers between devices, body(): lax.all_to_all(tangent, 'dp', split_axis=0, concat_axis=3, tiled=True)  53.2 us
    all_to_all x1, blocking collectives, body(): lax.all_to_all(arrived, 'dp', split_axis=3, concat_axis=0, tiled=True)  49.2 us
    unnamed x13, local copies, waits for them, and re-layouts  18.7 us
  transfers between devices with their start and end apart: 2, of which 2 were waited for; matrix products, arithmetic and copies ran while one was open for 0% of the time, Pallas kernels for 0%

profile of v1, /device:TPU:1, one launch (start us, length us, event | category | flops | bytes accessed | tf_op | source)
XLA Modules:
  0.0 798.3 jit_solution(13873935513218160869)
XLA Ops:
  0.0 7.0 stack.2
  7.0 566.8 %all_to_all.48 = bf16[32,128,1536]{2,1,0:T(8,128)(2,1)S(1)} all-to-all(bf16[32,128,1536]{2,1,0:T(8,128)(2,1)} %stack.2), channel_id=1, replica_groups=mesh['dp'=32,'expert'=16] {'dp'}, dimensions={0} | all-to-all | bytes 25165824 | tf_op jit(solution)/shard_map/all_to_all | solution.py:24
  573.8 4.6 copy-done.2
  578.4 3.9 convolution_convert_fusion
  582.3 1.4 copy.65
  583.7 4.1 all-to-all-start.1
  590.4 53.2 %all-to-all-done.1 = bf16[32,16,8,90]{3,2,1,0:T(8,128)(2,1)S(1)} async-done(((bf16[32,16,8,90]{3,2,1,0:T(8,128)(2,1)}), bf16[32,16,8,90]{3,2,1,0:T(8,128)(2,1)S(1)}, u32[]{:S(2)}, u32[]{:S(2)}) %all-to-all-start.1) | async-done | bytes 737312 | tf_op jit(solution)/shard_map/all_to_all | solution.py:34
  644.3 2.9 all_to_all.37
  647.1 6.8 all-to-all-start.2
  654.3 12.1 %all-to-all-done.2 = bf16[1,16,8,2880]{3,2,0,1:T(8,128)(2,1)S(1)} async-done(((bf16[1,16,8,2880]{3,2,0,1:T(8,128)(2,1)}), bf16[1,16,8,2880]{3,2,0,1:T(8,128)(2,1)S(1)}, u32[]{:S(2)}, u32[]{:S(2)}) %all-to-all-start.2) | async-done | bytes 737312 | tf_op jit(solution)/shard_map/all_to_all | solution.py:33
  666.4 3.7 gather_fusion
  670.1 4.7 gather.7
  674.8 6.3 multiply_reduce_fusion
  681.2 3.6 mul.54
  684.7 7.7 mul.55
  692.5 7.1 scatter_custom_fusion
  699.6 14.8 %all_to_all.49 = bf16[1,16,8,2880]{3,2,0,1:T(8,128)(2,1)S(1)} all-to-all(bf16[1,16,8,2880]{3,2,0,1:T(8,128)(2,1)S(1)} %bitcast.52), channel_id=1, replica_groups=mesh['dp'=32,'expert'=16] {'expert'}, dimensions={1} | all-to-all | bytes 1474560 | tf_op jit(solution)/shard_map/all_to_all | solution.py:54
  714.5 5.5 copy.69
  720.0 8.5 %reshape.152 = bf16[32,2,5760]{2,1,0:T(2,128)(2,1)S(1)} reshape(bf16[2880,1,8,16]{3,2,1,0:T(8,128)(2,1)} %bitcast.47) | data formatting | bytes 1474560
  728.5 49.2 %all_to_all.50 = bf16[32,2,5760]{2,1,0:T(2,128)(2,1)S(1)} all-to-all(bf16[32,2,5760]{2,1,0:T(2,128)(2,1)S(1)} %reshape.152), channel_id=1, replica_groups=mesh['dp'=32,'expert'=16] {'dp'}, dimensions={0} | all-to-all | bytes 1474560 | tf_op jit(solution)/shard_map/all_to_all | solution.py:55
  777.7 5.5 reshape.153
  783.2 6.5 copy.73
  790.2 6.8 convolution_bitcast_fusion
  797.0 1.4 copy.72
  (36 shorter events, 4.1 us)
Async XLA Ops:
  0.0 578.4 %copy-start = (bf16[1,90,1536]{2,1,0:T(8,128)(2,1)S(1)}, bf16[1,90,1536]{2,1,0:T(8,128)(2,1)}, u32[]{:S(2)}) copy-start(bf16[1,90,1536]{2,1,0:T(8,128)(2,1)} %param.5) | copy-start | bytes 829444
  573.8 4.6 copy-start.2
  582.3 5.5 copy-start.3
  583.7 59.9 %all-to-all-start.1 = ((bf16[32,16,8,90]{3,2,1,0:T(8,128)(2,1)}), bf16[32,16,8,90]{3,2,1,0:T(8,128)(2,1)S(1)}, u32[]{:S(2)}, u32[]{:S(2)}) async-start(bf16[32,16,8,90]{3,2,1,0:T(8,128)(2,1)} %bitcast.4), calls=%async_computation.1 | async-start | bytes 2097152 | tf_op jit(solution)/shard_map/all_to_all | solution.py:34
  588.2 65.8 %copy-start.4 = (f32[128,4]{0,1:T(4,128)S(1)}, f32[128,4]{0,1:T(4,128)}, u32[]{:S(2)}) copy-start(f32[128,4]{0,1:T(4,128)} %param.7) | copy-start | bytes 6148
  647.1 19.3 %all-to-all-start.2 = ((bf16[1,16,8,2880]{3,2,0,1:T(8,128)(2,1)}), bf16[1,16,8,2880]{3,2,0,1:T(8,128)(2,1)S(1)}, u32[]{:S(2)}, u32[]{:S(2)}) async-start(bf16[1,16,8,2880]{3,2,0,1:T(8,128)(2,1)} %bitcast.7), calls=%async_computation.2 | async-start | bytes 1507328 | tf_op jit(solution)/shard_map/all_to_all | solution.py:33
  790.2 8.2 %copy-start.1 = (bf16[1,90,1536]{2,1,0:T(8,128)(2,1)S(1)}, bf16[1,90,1536]{2,1,0:T(8,128)(2,1)}, u32[]{:S(2)}) copy-start(bf16[1,90,1536]{2,1,0:T(8,128)(2,1)} %param.5) | copy-start | bytes 829444
